TPU v7x, 256 devices: a whole 4x4x8 slice. The times are simulated.
256 devices in a mesh: blk: 64 (over x, z, y_hi), col: 4 (over y_lo, core).
Axes of the slice: x: 4, y: 4 (y_hi: 2, y_lo: 2; y = y_hi * 2 + y_lo), z: 8, core: 2. Of those that a mesh axis runs over, the one named last changes fastest.
Arguments:
- points: bfloat16 [32768, 128], P(('blk', 'col')), may hold values from -4.5 to 4.5
- targets: float32 [32768, 32], P(('blk', 'col')), may hold values from -6 to 6
- pivots: int32 [2, 256], replicated, may hold values from 0 to 32767, as said below
Outputs:
- factor: bfloat16 [32768, 512], P(('blk', 'col'))
- solution: float32 [32768, 32], P(('blk', 'col'))
- residual: float32 [32768, 32], P(('blk', 'col'))
Inputs may be any that keep to these rules, and one draw needn't show every extreme that they name: `pivots`: the 512 indices are distinct; 0 and 32767 are among them.
All inputs are finite; a program needn't handle non-finite values.
Results may differ from a plain program's by a relative error of at most 0.012.
Values may be sent and summed in bfloat16 or wider, within the bound.
No kernel may reach another device: no remote copies, remote signals or barrier semaphores. Data moves between devices by JAX's collectives and lax.ppermute only.
A program may use at most 64 MiB of HBM per device.

v0:
```python
import jax
import jax.numpy as jnp
from jax import lax
from jax.sharding import PartitionSpec as P

FEATURES = 128
ITERS = 3


noise_level = 0.5
jitter_level = 0.05
highest = lax.Precision.HIGHEST


def squared_norms(point_rows):
    wide_rows = point_rows.astype(jnp.float32)
    return jnp.sum(wide_rows * wide_rows, axis=1)


def kernel_block(left_rows, left_norms, right_rows, right_norms):
    inner = lax.dot_general(
        left_rows, right_rows, (((1,), (1,)), ((), ())), preferred_element_type=jnp.float32
    )
    distance = left_norms[:, None] + right_norms[None, :] - 2.0 * inner
    return jnp.exp(-2.0 * distance / FEATURES)


def lower_solve(lower_factor, right_rows):
    return jax.scipy.linalg.solve_triangular(lower_factor, right_rows.T, lower=True).T


def build_factor(point_rows, first_pick, second_pick):
    row_norms = squared_norms(point_rows)
    first_norms = squared_norms(first_pick)
    second_norms = squared_norms(second_pick)
    identity_piv = jnp.eye(first_pick.shape[0], dtype=jnp.float32)
    first_chol = jnp.linalg.cholesky(
        kernel_block(first_pick, first_norms, first_pick, first_norms) + jitter_level * identity_piv
    )
    first_coef = lower_solve(
        first_chol, kernel_block(point_rows, row_norms, first_pick, first_norms)
    )
    shared_coef = lower_solve(
        first_chol, kernel_block(second_pick, second_norms, first_pick, first_norms)
    )
    schur_block = (
        kernel_block(second_pick, second_norms, second_pick, second_norms)
        + jitter_level * identity_piv
        - jnp.dot(shared_coef, shared_coef.T, precision=highest)
    )
    second_chol = jnp.linalg.cholesky(schur_block)
    second_cross = kernel_block(point_rows, row_norms, second_pick, second_norms) - jnp.dot(
        first_coef, shared_coef.T, precision=highest
    )
    second_coef = lower_solve(second_chol, second_cross)
    return jnp.concatenate([first_coef, second_coef], axis=1)


def per_device(points, targets, pivots):
    row_count = points.shape[0]
    piv_count = pivots.shape[1]
    shard_index = lax.axis_index("blk") * lax.axis_size("col") + lax.axis_index("col")
    first_row = shard_index * row_count
    flat_pivots = pivots.reshape(-1)
    owned = (
        flat_pivots[:, None] == first_row + jnp.arange(row_count, dtype=jnp.int32)[None, :]
    ).astype(jnp.float32)
    local_pick = jnp.dot(owned, points.astype(jnp.float32), precision=highest)
    picked = lax.psum(local_pick, ("blk", "col")).astype(jnp.bfloat16)
    wide_factor = build_factor(points, picked[:piv_count], picked[piv_count:])
    factor = wide_factor.astype(jnp.bfloat16)
    local_gram = lax.dot_general(
        wide_factor, wide_factor, (((0,), (0,)), ((), ())), precision=highest
    )
    gram = lax.psum(local_gram, ("blk", "col"))
    gram = gram + noise_level * jnp.eye(2 * piv_count, dtype=jnp.float32)
    gram_chol = jnp.linalg.cholesky(gram)

    def precondition(residual_now):
        local_proj = lax.dot_general(
            wide_factor, residual_now, (((0,), (0,)), ((), ())), precision=highest
        )
        projection = lax.psum(local_proj, ("blk", "col"))
        coefficients = jax.scipy.linalg.cho_solve((gram_chol, True), projection)
        scaled = (
            residual_now - jnp.dot(wide_factor, coefficients, precision=highest)
        ) / noise_level
        return (scaled, lax.psum(jnp.sum(residual_now * scaled, axis=0), ("blk", "col")))

    own_block = lax.all_gather(points, "col", axis=0, tiled=True)
    own_norms = squared_norms(own_block)

    def tile_add(total, key_rows, key_norms, direction_rows):
        weights = kernel_block(own_block, own_norms, key_rows, key_norms)
        return total + jnp.dot(weights, direction_rows, precision=highest)

    solution = jnp.zeros_like(targets)
    residual = targets
    direction_now, inner_now = precondition(residual)
    for step_index in range(ITERS):
        empty = jnp.zeros((own_block.shape[0], direction_now.shape[1]), jnp.float32)
        add_key_rows = lax.all_gather(points.astype(jnp.float32), "blk", axis=0, tiled=True).astype(
            jnp.bfloat16
        )
        fold_direction_rows = lax.all_gather(direction_now, "blk", axis=0, tiled=True)
        piece_rows = add_key_rows.shape[0]
        splits = piece_rows // row_count

        def scan_step(carry, operands):
            return (tile_add(carry, operands[0], operands[1], operands[2]), None)

        stacked = (
            add_key_rows.reshape(splits, row_count, add_key_rows.shape[1]),
            squared_norms(add_key_rows).reshape(splits, row_count),
            fold_direction_rows.reshape(splits, row_count, fold_direction_rows.shape[1]),
        )
        result, unused = lax.scan(scan_step, empty, stacked)
        image = (
            lax.psum_scatter(result, "col", scatter_dimension=0, tiled=True)
            + noise_level * direction_now
        )
        curvature = lax.psum(jnp.sum(direction_now * image, axis=0), ("blk", "col"))
        step_size = inner_now / curvature
        solution = solution + step_size * direction_now
        residual = residual - step_size * image
        if step_index + 1 < ITERS:
            scaled, inner_next = precondition(residual)
            direction_now = scaled + inner_next / inner_now * direction_now
            inner_now = inner_next
    return (factor, solution, residual)


def solution(mesh):
    return jax.shard_map(
        per_device,
        mesh=mesh,
        in_specs=(P(("blk", "col"), None), P(("blk", "col"), None), P()),
        out_specs=(P(("blk", "col"), None), P(("blk", "col"), None), P(("blk", "col"), None)),
        check_vma=False,
    )
```

profile of v0, /device:TPU:1, one launch (start us, length us, event | category | flops | bytes accessed | tf_op | source)
XLA Modules:
  0.0 2410.5 jit_solution(17141482593332180947)
XLA Ops:
  8.9 82.6 %all-reduce.14 = bf16[512,128]{1,0:T(8,128)(2,1)S(1)} all-reduce(f32[512,128]{1,0:T(8,128)S(1)} %fusion.57), channel_id=1, replica_groups=mesh['blk'=64,'col'=4] {'blk','col'}, use_global_device_ids=true, to_apply=%region_0.0 | all-reduce | flops 65536 | bytes 393216 | tf_op jit(solution)/shard_map/psum | solution.py:69
  92.1 11.7 cholesky.354
  114.3 11.7 cholesky.364
  133.6 19.7 custom-call.55
  156.1 11.7 cholesky.381
  178.1 11.7 cholesky.391
  196.9 19.7 custom-call.57
  221.1 251.4 %all-reduce.13.cloned.1.call-done = (f32[512,512]{1,0:T(8,128)}, f32[512,32]{0,1:T(8,128)}) async-done(((f32[512,512]{1,0:T(8,128)}, f32[512,32]{0,1:T(8,128)}), (f32[512,512]{1,0:T(8,128)}, f32[512,32]{0,1:T(8,128)})) %all-reduce.13.cloned.1.call-update) | async-done | bytes 1114128 | tf_op jit(solution)/shard_map/psum | solution.py:75
  474.5 11.7 cholesky.166
  496.9 11.7 cholesky.189
  509.9 10.0 custom-call.43
  520.5 11.7 cholesky.292
  543.4 11.7 cholesky.305
  558.7 10.4 while.55
  569.1 40.1 %custom-call.59 = f32[4,128,128]{1,2,0:T(8,128)S(1)} custom-call(f32[4,128,128]{2,1,0:T(8,128)} %get-tuple-element.393), custom_call_target="InvertDiagBlocksLowerTriangular" | custom-call | tf_op jit(solution)/shard_map/jit(_cho_solve)/triangular_solve | solution.py:84
  621.0 92.2 %all-gather.7.cloned.1.call-done = f32[8192,32]{0,1:T(8,128)} async-done(((f32[128,32]{0,1:T(8,128)}), f32[8192,32]{0,1:T(8,128)}) %all-gather.7.cloned.1.call-update) | async-done | bytes 1048592 | tf_op jit(solution)/shard_map/all_gather | solution.py:105
  716.7 116.0 %all-gather.5.cloned.1.call-done = bf16[8192,128]{1,0:T(8,128)(2,1)} async-done(((bf16[128,128]{1,0:T(8,128)(2,1)}), bf16[8192,128]{1,0:T(8,128)(2,1)}) %all-gather.5.cloned.1.call-update) | async-done | bytes 2097168 | tf_op jit(solution)/shard_map/all_gather | solution.py:102
  835.5 144.7 %while.50 = (s32[]{:T(128)}, f32[512,32]{0,1:T(8,128)S(1)}, f32[512]{0:T(512)S(1)}, f32[64,128]{1,0:T(8,128)S(1)}, bf16[64,128,128]{2,1,0:T(8,128)(2,1)}, /*inde...) while((s32[]{:T(128)}, f32[512,32]{0,1:T(8,128)S(1)}, ...), condition=%wide.region_23.28_spmd.clone, body=%wide.region_22.27_spmd.clone.sunk | while | flops 42237952 | bytes 889451 | solution.py:117
  980.9 20.1 reduce-scatter.4.cloned.1.call-done
  1001.8 77.0 %all-reduce.2 = (f32[32]{0:T(128)S(1)}, f32[32]{0:T(128)S(1)}) all-reduce(f32[32]{0:T(128)S(1)} %get-tuple-element.431, f32[32]{0:T(128)S(1)} %get-tuple-element.430), channel_id=1, replica_groups=mesh['blk'=64,'col'=4] {'blk','col'}, use_global_device_ids=true, to_apply=%region_19.24 | all-reduce | flops 64 | bytes 512 | tf_op jit(solution)/shard_map/psum | solution.py:88
  1079.9 234.4 %all-reduce.9.cloned.1.call-done = f32[512,32]{0,1:T(8,128)} async-done(((f32[512,32]{0,1:T(8,128)}), f32[512,32]{0,1:T(8,128)}) %all-reduce.9.cloned.1.call-update) | async-done | bytes 65552 | tf_op jit(solution)/shard_map/psum | solution.py:83
  1320.8 74.4 %psum.83 = f32[32]{0:T(128)S(1)} all-reduce(f32[32]{0:T(128)S(1)} %get-tuple-element.537), channel_id=1, replica_groups=mesh['blk'=64,'col'=4] {'blk','col'}, use_global_device_ids=true, to_apply=%region_29.34 | all-reduce | flops 32 | bytes 256 | tf_op jit(solution)/shard_map/psum | solution.py:88
  1396.0 95.6 %all-gather.9.cloned.1.call-done = f32[8192,32]{0,1:T(8,128)} async-done(((f32[128,32]{0,1:T(8,128)}), f32[8192,32]{0,1:T(8,128)}) %all-gather.9.cloned.1.call-update) | async-done | bytes 1048592 | tf_op jit(solution)/shard_map/all_gather | solution.py:105
  1495.1 144.7 %while.51 = (s32[]{:T(128)}, f32[512,32]{0,1:T(8,128)S(1)}, f32[512]{0:T(512)S(1)}, f32[64,128]{1,0:T(8,128)S(1)}, bf16[64,128,128]{2,1,0:T(8,128)(2,1)}, /*inde...) while((s32[]{:T(128)}, f32[512,32]{0,1:T(8,128)S(1)}, ...), condition=%wide.region_31.36_spmd.clone, body=%wide.region_30.35_spmd.clone.sunk | while | flops 42237952 | bytes 889451 | solution.py:117
  1640.5 21.1 reduce-scatter.6.cloned.1.call-done
  1662.4 77.3 %psum.84 = f32[32]{0:T(128)S(1)} all-reduce(f32[32]{0:T(128)S(1)} %multiply_reduce_fusion.7), channel_id=1, replica_groups=mesh['blk'=64,'col'=4] {'blk','col'}, use_global_device_ids=true, to_apply=%region_34.39 | all-reduce | flops 32 | bytes 256 | tf_op jit(solution)/shard_map/psum | solution.py:122
  1741.6 234.4 %all-reduce.11.cloned.1.call-done = f32[512,32]{0,1:T(8,128)} async-done(((f32[512,32]{0,1:T(8,128)}), f32[512,32]{0,1:T(8,128)}) %all-reduce.11.cloned.1.call-update) | async-done | bytes 65552 | tf_op jit(solution)/shard_map/psum | solution.py:83
  1982.4 74.4 %psum.86 = f32[32]{0:T(128)S(1)} all-reduce(f32[32]{0:T(128)S(1)} %get-tuple-element.539), channel_id=1, replica_groups=mesh['blk'=64,'col'=4] {'blk','col'}, use_global_device_ids=true, to_apply=%region_37.42 | all-reduce | flops 32 | bytes 256 | tf_op jit(solution)/shard_map/psum | solution.py:88
  2057.6 95.6 %all-gather.11.cloned.1.call-done = f32[8192,32]{0,1:T(8,128)} async-done(((f32[128,32]{0,1:T(8,128)}), f32[8192,32]{0,1:T(8,128)}) %all-gather.11.cloned.1.call-update) | async-done | bytes 1048592 | tf_op jit(solution)/shard_map/all_gather | solution.py:105
  2156.8 144.7 %while.52 = (s32[]{:T(128)}, f32[512,32]{0,1:T(8,128)S(1)}, f32[512]{0:T(512)S(1)}, f32[64,128]{1,0:T(8,128)S(1)}, bf16[64,128,128]{2,1,0:T(8,128)(2,1)}, /*inde...) while((s32[]{:T(128)}, f32[512,32]{0,1:T(8,128)S(1)}, ...), condition=%wide.region_39.44_spmd.clone, body=%wide.region_38.43_spmd.clone.sunk | while | flops 42237952 | bytes 889451 | solution.py:117
  2302.1 21.1 reduce-scatter.8.cloned.1.call-done
  2324.8 77.0 %psum.87 = f32[32]{0:T(128)S(1)} all-reduce(f32[32]{0:T(128)S(1)} %multiply_reduce_fusion.5), channel_id=1, replica_groups=mesh['blk'=64,'col'=4] {'blk','col'}, use_global_device_ids=true, to_apply=%region_42.47 | all-reduce | flops 32 | bytes 256 | tf_op jit(solution)/shard_map/psum | solution.py:122
  (799 shorter events, 562.2 us)
Async XLA Ops:
  7.2 119.0 %copy-start.5 = (bf16[128,128]{1,0:T(8,128)(2,1)S(1)}, bf16[128,128]{1,0:T(8,128)(2,1)}, u32[]{:S(2)}) copy-start(bf16[128,128]{1,0:T(8,128)(2,1)} %param.16) | copy-start | bytes 98308
  7.2 465.3 %all-reduce.13.cloned.1.call-start = ((), (), s32[]{:S(2)}) async-start(), calls=%async_computation.12 | async-start | bytes 2228224 | tf_op jit(solution)/shard_map/psum | solution.py:75
  154.5 65.5 %copy-start.8 = (f32[128,32]{0,1:T(8,128)S(1)}, f32[128,32]{0,1:T(8,128)}, u32[]{:S(2)}) copy-start(f32[128,32]{0,1:T(8,128)} %param.17) | copy-start | bytes 49156
  221.1 492.1 %all-gather.7.cloned.1.call-start = ((), (), s32[]{:S(2)}) async-start(), calls=%async_computation.4 | async-start | bytes 1064960 | tf_op jit(solution)/shard_map/all_gather | solution.py:105
  472.5 1.8 copy-start
  474.5 134.7 %copy-start.9 = (f32[512,32]{0,1:T(8,128)S(1)}, f32[512,32]{0,1:T(8,128)}, u32[]{:S(2)}) copy-start(f32[512,32]{0,1:T(8,128)} %get-tuple-element.501) | copy-start | bytes 196612
  496.5 117.6 %copy-start.6 = (bf16[128,128]{1,0:T(8,128)(2,1)S(1)}, bf16[128,128]{1,0:T(8,128)(2,1)}, u32[]{:S(2)}) copy-start(bf16[128,128]{1,0:T(8,128)(2,1)} %param.16) | copy-start | bytes 98308
  613.3 219.4 %all-gather.5.cloned.1.call-start = ((), (), s32[]{:S(2)}) async-start(), calls=%async_computation.3 | async-start | bytes 2129920 | tf_op jit(solution)/shard_map/all_gather | solution.py:102
  614.1 386.8 %reduce-scatter.4.cloned.1.call-start = ((), (), s32[]{:S(2)}) async-start(), calls=%async_computation.5 | async-start | bytes 81920 | tf_op jit(solution)/shard_map/reduce_scatter | solution.py:119
  980.2 0.6 copy-start.1
  980.8 333.5 %all-reduce.9.cloned.1.call-start = ((), (), s32[]{:S(2)}) async-start(), calls=%async_computation.6 | async-start | bytes 131072 | tf_op jit(solution)/shard_map/psum | solution.py:83
  1079.9 411.7 %all-gather.9.cloned.1.call-start = ((), (), s32[]{:S(2)}) async-start(), calls=%async_computation.7 | async-start | bytes 1064960 | tf_op jit(solution)/shard_map/all_gather | solution.py:105
  1395.9 265.7 %reduce-scatter.6.cloned.1.call-start = ((), (), s32[]{:S(2)}) async-start(), calls=%async_computation.8 | async-start | bytes 81920 | tf_op jit(solution)/shard_map/reduce_scatter | solution.py:119
  1396.0 265.6 %copy-start.4 = (f32[128,32]{0,1:T(8,128)S(1)}, f32[128,32]{0,1:T(8,128)}, u32[]{:S(2)}) copy-start(f32[128,32]{0,1:T(8,128)} %multiply_add_fusion.4) | copy-start | bytes 49156
  1639.8 0.6 copy-start.2
  1640.5 335.5 %all-reduce.11.cloned.1.call-start = ((), (), s32[]{:S(2)}) async-start(), calls=%async_computation.9 | async-start | bytes 131072 | tf_op jit(solution)/shard_map/psum | solution.py:83
  1741.5 411.7 %all-gather.11.cloned.1.call-start = ((), (), s32[]{:S(2)}) async-start(), calls=%async_computation.10 | async-start | bytes 1064960 | tf_op jit(solution)/shard_map/all_gather | solution.py:105
  2057.5 265.7 %reduce-scatter.8.cloned.1.call-start = ((), (), s32[]{:S(2)}) async-start(), calls=%async_computation.11 | async-start | bytes 81920 | tf_op jit(solution)/shard_map/reduce_scatter | solution.py:119
  2057.6 265.6 %copy-start.7 = (f32[128,32]{0,1:T(8,128)S(1)}, f32[128,32]{0,1:T(8,128)}, u32[]{:S(2)}) copy-start(f32[128,32]{0,1:T(8,128)} %multiply_add_fusion.2) | copy-start | bytes 49156
  2301.4 0.6 copy-start.3
Sparse Core Ops, SparseCore 0:
  221.2 251.2 all-reduce.12
  613.5 99.6 all-gather.6
  717.3 115.3 all-gather.4
  981.0 19.9 reduce-scatter.3
  1080.0 234.2 all-reduce.8
  1396.0 95.4 all-gather.8
  1640.6 20.9 reduce-scatter.5
  1741.6 234.2 all-reduce.10
  2057.6 95.4 all-gather.10
  2302.2 20.9 reduce-scatter.7
where the time goes:
time: 2440 us; the launch traced here: 2410 us
  waiting for transfers between devices  1180 us (48%)
  blocking collectives  469 us (19%)
  matrix products  455 us (19%)
  other arithmetic  239 us (10%)
  local copies, waits for them, and re-layouts  35.5 us (1%)
    psum x2, waiting for transfers between devices, precondition(): projection = lax.psum(local_proj, ('blk', 'col'))  469 us
    all_gather x3, waiting for transfers between devices, per_device(): lax.all_gather(direction_now, 'blk', axis=0, tiled=True)  283 us
    psum x1, waiting for transfers between devices, per_device(): gram = lax.psum(local_gram, ('blk', 'col'))  251 us
    dot_general x192, matrix products, tile_add(): return total + jnp.dot(weights, direction_rows, precision=highest)  238 us
    psum x3, blocking collectives, precondition(): lax.psum(jnp.sum(residual_now * scaled, axis=0), ('blk', 'col'))  226 us
    dot_general x197, matrix products, kernel_block(): lax.dot_general(left_rows, right_rows, (((1,), (1,)), ((), ())), preferre...  187 us
    psum x2, blocking collectives, per_device(): curvature = lax.psum(jnp.sum(direction_now * image, axis=0), ('blk', 'col'))  154 us
    all_gather x1, waiting for transfers between devices, per_device(): lax.all_gather(points.astype(jnp.float32), 'blk', axis=0, tiled=True)  116 us
  transfers between devices with their start and end apart: 10, of which 10 were waited for; matrix products, arithmetic and copies ran while one was open for 0% of the time, Pallas kernels for 0%

commit v1 on v0

v1 whole, which is shorter than its diff:
```python
import functools

import jax
import jax.numpy as jnp
import numpy as np
from jax import lax
from jax.experimental import pallas as pl
from jax.experimental.pallas import tpu as pltpu
from jax.sharding import Mesh, PartitionSpec as P

ITERS = 3
NOISE = 0.5
JITTER = 0.05
HIGHEST = lax.Precision.HIGHEST
INTERPRET = False

U = ("z", "yh")
V = ("x", "yl", "c")
ALL = ("x", "z", "yh", "yl", "c")


def swap(blocks, axes):
    return lax.all_to_all(blocks, axes, 0, 0, tiled=False)


def share(block, axes):
    count = lax.axis_size(axes)
    return swap(jnp.broadcast_to(block[None], (count,) + block.shape), axes)


def three_parts(values):
    high = lax.reduce_precision(values, 8, 7)
    rest = values - high
    middle = lax.reduce_precision(rest, 8, 7)
    low = rest - middle
    return [part.astype(jnp.bfloat16) for part in (high, middle, low)]


def augment(rows):
    wide = rows.astype(jnp.float32)
    halves = three_parts(jnp.sum(wide * wide, axis=1, keepdims=True) * (-1.0 / 64.0))
    ones = [jnp.ones_like(halves[0])] * 3
    pad = jnp.zeros((rows.shape[0], 122), jnp.bfloat16)
    left = jnp.concatenate([(wide * 0.03125).astype(jnp.bfloat16)] + halves + ones + [pad], axis=1)
    right = jnp.concatenate([rows] + ones + halves + [pad], axis=1)
    return left, right


def dot_nt(left, right, precision=None):
    return lax.dot_general(
        left, right, (((1,), (1,)), ((), ())), precision=precision, preferred_element_type=jnp.float32
    )


def kernel_of(left, right):
    return jnp.exp(dot_nt(left, right))


def product_body(chunk, key_ref, row_ref, parts_ref, out_ref):
    keys = key_ref.shape[0]
    columns = out_ref.shape[0]
    total = jnp.zeros(out_ref.shape, jnp.float32)
    for start in range(0, keys, chunk):
        values = jnp.exp(dot_nt(key_ref[start:start + chunk, :], row_ref[...]))
        high = values.astype(jnp.bfloat16)
        low = (values - high.astype(jnp.float32)).astype(jnp.bfloat16)
        wide = jnp.dot(parts_ref[:, start:start + chunk], high, preferred_element_type=jnp.float32)
        narrow = jnp.dot(
            parts_ref[:2 * columns, start:start + chunk], low, preferred_element_type=jnp.float32
        )
        total = total + (
            wide[:columns] + wide[columns:2 * columns] + wide[2 * columns:]
            + narrow[:columns] + narrow[columns:]
        )
    out_ref[...] = total


def kernel_product(key_left, row_right, direction):
    keys, depth = key_left.shape
    rows = row_right.shape[0]
    columns = direction.shape[0]
    parts = jnp.concatenate(three_parts(direction), axis=0)
    block = min(256, rows)
    return pl.pallas_call(
        functools.partial(product_body, min(256, keys)),
        grid=(rows // block,),
        in_specs=[
            pl.BlockSpec((keys, depth), lambda i: (0, 0)),
            pl.BlockSpec((block, depth), lambda i: (i, 0)),
            pl.BlockSpec((3 * columns, keys), lambda i: (0, 0)),
        ],
        out_specs=pl.BlockSpec((columns, block), lambda i: (0, i)),
        out_shape=jax.ShapeDtypeStruct((columns, rows), jnp.float32),
        compiler_params=pltpu.CompilerParams(vmem_limit_bytes=32 << 20),
        interpret=INTERPRET,
        name="kernel_product",
    )(key_left, row_right, parts)


def inverse_factor(matrix):
    order = matrix.shape[0]
    lower = jnp.linalg.cholesky(matrix)
    return jax.scipy.linalg.solve_triangular(lower, jnp.eye(order, dtype=jnp.float32), lower=True)


def per_device(points, targets, pivots):
    own = points.shape[0]
    columns = targets.shape[1]
    u_size, v_size = lax.axis_size(U), lax.axis_size(V)
    u_at, v_at = lax.axis_index(U), lax.axis_index(V)
    flat_pivots = pivots.reshape(-1)
    piv = flat_pivots.shape[0]
    lanes = 128

    packed = share(jnp.concatenate([points.astype(jnp.float32), targets.T], axis=0), U)
    key_points = packed[:, :own].astype(jnp.bfloat16).reshape(u_size * own, -1)
    residual = packed[:, own:].transpose(1, 0, 2).reshape(columns, u_size * own)

    sizes = {axis: lax.axis_size(axis) for axis in ALL}
    place = jnp.zeros((), jnp.int32)
    u_rest = jnp.arange(u_size, dtype=jnp.int32)
    u_index = {}
    for axis in reversed(U):
        u_index[axis] = u_rest % sizes[axis]
        u_rest = u_rest // sizes[axis]
    for axis in ALL:
        place = place * sizes[axis] + (u_index[axis] if axis in U else lax.axis_index(axis))
    key_ids = (place[:, None] * own + jnp.arange(own, dtype=jnp.int32)[None, :]).reshape(1, -1)

    owned = (flat_pivots[:, None] == key_ids).astype(jnp.bfloat16)
    held = jnp.dot(owned, key_points, preferred_element_type=jnp.float32).astype(jnp.bfloat16)
    part = piv // v_size
    packed = swap(
        jnp.concatenate(
            [
                jnp.broadcast_to(points[None], (v_size,) + points.shape),
                held.reshape(v_size, part, -1),
            ],
            axis=1,
        ),
        V,
    )
    row_points = packed[:, :own].reshape(v_size * own, -1)
    picked = jnp.sum(packed[:, own:].astype(jnp.float32), axis=0).astype(jnp.bfloat16)
    picked = share(picked, V).reshape(piv, -1)

    piv_left, piv_right = augment(picked)
    key_left, key_right = augment(key_points)
    _, row_right = augment(row_points)

    identity = jnp.eye(piv, dtype=jnp.float32)
    low_inverse = inverse_factor(kernel_of(piv_left, piv_right) + JITTER * identity)

    def wide_of(left):
        return dot_nt(kernel_of(left, piv_right), low_inverse, HIGHEST)

    key_wide = wide_of(key_left)
    factor = lax.dynamic_slice_in_dim(key_wide, u_at * own, own, 0).astype(jnp.bfloat16)

    local_gram = lax.dot_general(
        key_wide, key_wide, (((0,), (0,)), ((), ())), precision=HIGHEST
    )
    local_proj = jnp.dot(residual, key_wide, precision=HIGHEST)
    local_sums = jnp.sum(residual * residual, axis=1)
    tail = jnp.zeros((8 * lanes,), jnp.float32).at[:columns].set(local_sums).reshape(1, 8, lanes)
    packed = swap(
        jnp.concatenate(
            [
                local_gram.reshape(v_size, -1, lanes),
                local_proj.reshape(v_size, -1, lanes),
                jnp.broadcast_to(tail, (v_size, 8, lanes)),
            ],
            axis=1,
        ),
        V,
    )
    packed = share(jnp.sum(packed, axis=0), V)
    gram_rows = piv * piv // v_size // lanes
    proj_rows = columns * piv // v_size // lanes
    gram = packed[:, :gram_rows].reshape(piv, piv) + NOISE * identity
    projection = packed[:, gram_rows:gram_rows + proj_rows].reshape(columns, piv)
    squares = packed[0, gram_rows + proj_rows:].reshape(-1)[:columns]
    gram_inverse = inverse_factor(gram)

    def gram_solve(proj):
        return jnp.dot(dot_nt(proj, gram_inverse, HIGHEST), gram_inverse, precision=HIGHEST)

    def precondition(res, coef):
        return (res - dot_nt(coef, key_wide, HIGHEST)) / NOISE

    def own_part(values):
        return lax.dynamic_slice_in_dim(values, u_at * own, own, 1)

    coefficients = gram_solve(projection)
    direction = precondition(residual, coefficients)
    inner = (squares - jnp.sum(projection * coefficients, axis=1)) / NOISE
    solution_own = jnp.zeros((columns, own), jnp.float32)
    for step in range(ITERS):
        last = step + 1 == ITERS
        direction_own = own_part(direction)
        partial = kernel_product(key_left, row_right, direction)
        blocks = partial.reshape(columns, v_size, own).transpose(1, 0, 2)
        image_own = jnp.sum(swap(blocks, V), axis=0) + NOISE * direction_own
        if last:
            curve = jnp.sum(direction_own * image_own, axis=1)
            curve = jnp.zeros((8 * lanes,), jnp.float32).at[:columns].set(curve).reshape(8, lanes)
            curve = jnp.sum(share(curve, V), axis=0)
            curve = jnp.sum(share(curve, U), axis=0)
            alpha = (inner / curve.reshape(-1)[:columns])[:, None]
            solution_own = solution_own + alpha * direction_own
            residual_own = own_part(residual) - alpha * image_own
            break
        image = share(image_own, U).transpose(1, 0, 2).reshape(columns, u_size * own)
        image_proj = jnp.dot(image, key_wide, precision=HIGHEST)
        sums = jnp.concatenate(
            [
                jnp.sum(direction * image, axis=1),
                jnp.sum(residual * image, axis=1),
                jnp.sum(image * image, axis=1),
            ]
        )
        sums = jnp.zeros((8 * lanes,), jnp.float32).at[:3 * columns].set(sums).reshape(8, lanes)
        packed = jnp.sum(
            share(jnp.concatenate([image_proj.reshape(-1, lanes), sums], axis=0), V), axis=0
        )
        image_proj = packed[:-8].reshape(columns, piv)
        sums = packed[-8:].reshape(-1)
        curve, cross, image_squares = (
            sums[:columns], sums[columns:2 * columns], sums[2 * columns:3 * columns]
        )
        alpha = inner / curve
        squares = squares - 2.0 * alpha * cross + alpha * alpha * image_squares
        solution_own = solution_own + alpha[:, None] * direction_own
        residual = residual - alpha[:, None] * image
        projection = projection - alpha[:, None] * image_proj
        coefficients = gram_solve(projection)
        inner_next = (squares - jnp.sum(projection * coefficients, axis=1)) / NOISE
        beta = (inner_next / inner)[:, None]
        inner = inner_next
        direction = precondition(residual, coefficients) + beta * direction
    return (factor, solution_own.T, residual_own.T)


def solution(mesh):
    shape = mesh.devices.shape
    if shape == (64, 4):
        grid = Mesh(mesh.devices.reshape(4, 8, 2, 2, 2), ALL)
    else:
        grid = Mesh(mesh.devices.reshape(2, 2, 2, 2, 1), ALL)
    return jax.shard_map(
        per_device,
        mesh=grid,
        in_specs=(P(ALL, None), P(ALL, None), P()),
        out_specs=(P(ALL, None), P(ALL, None), P(ALL, None)),
        check_vma=False,
    )
```

time: 2440 us -> 740 us (0.30)
  waiting for transfers between devices: 1180 us -> 90.3 us
  blocking collectives: 469 us -> 83.6 us
  matrix products: 455 us -> 99.3 us
  other arithmetic: 239 us -> 292 us
  local copies, waits for them, and re-layouts: 35.5 us -> 87 us
  starting transfers between devices: 0.41 us -> 51 us
    psum x3 -> x0, waiting for transfers between devices: 720 us -> none  [the longest x2 469 us: precondition(): projection = lax.psum(local_proj, ('blk', 'col'))]
    psum x6 -> x0, blocking collectives: 463 us -> none  [the longest x3 226 us: precondition(): lax.psum(jnp.sum(residual_now * scaled, axis=0), ('blk', 'col'))]
    all_gather x4 -> x0, waiting for transfers between devices: 399 us -> none  [the longest x3 283 us: per_device(): lax.all_gather(direction_now, 'blk', axis=0, tiled=True)]
    dot_general x399 -> x17, matrix products: 434 us -> 57.7 us  [the longest x9 32.1 us: dot_nt(): lax.dot_general(left, right, (((1,), (1,)), ((), ())), precision=precisio...]
    all_to_all x0 -> x8, waiting for transfers between devices: none -> 90.3 us  [swap(): return lax.all_to_all(blocks, axes, 0, 0, tiled=False)]
    all_to_all x0 -> x6, blocking collectives: none -> 83.6 us  [swap(): return lax.all_to_all(blocks, axes, 0, 0, tiled=False)]
    reduce_scatter x3 -> x0, waiting for transfers between devices: 62.2 us -> none  [per_device(): lax.psum_scatter(result, 'col', scatter_dimension=0, tiled=True)]
    all_to_all x0 -> x8, starting transfers between devices: none -> 51 us  [swap(): return lax.all_to_all(blocks, axes, 0, 0, tiled=False)]
  transfers between devices with their start and end apart: 10 -> 8, of which waited for: 10 -> 7; matrix products, arithmetic and copies ran while one was open for 0% -> 4% of each run, Pallas kernels for 0% -> 0%
where the time goes in v1:
time: 740 us; the launch traced here: 733 us
  other arithmetic  292 us (39%)
  matrix products  99.3 us (13%)
  waiting for transfers between devices  90.3 us (12%)
  local copies, waits for them, and re-layouts  87 us (12%)
  blocking collectives  83.6 us (11%)
  starting transfers between devices  51 us (7%)
  Pallas kernels  23.1 us (3%)
    another operation x29, other arithmetic, inverse_factor(): lower = jnp.linalg.cholesky(matrix)  172 us
    all_to_all x8, waiting for transfers between devices, swap(): return lax.all_to_all(blocks, axes, 0, 0, tiled=False)  90.3 us
    another operation x5, other arithmetic, inverse_factor(): jax.scipy.linalg.solve_triangular(lower, jnp.eye(order, dtype=jnp.float32...  86.8 us
    all_to_all x6, blocking collectives, swap(): return lax.all_to_all(blocks, axes, 0, 0, tiled=False)  83.6 us
    all_to_all x8, starting transfers between devices, swap(): return lax.all_to_all(blocks, axes, 0, 0, tiled=False)  51 us
    dot_general x9, matrix products, dot_nt(): lax.dot_general(left, right, (((1,), (1,)), ((), ())), precision=precisio...  32.1 us
    another operation x27, local copies, waits for them, and re-layouts, inverse_factor(): jax.scipy.linalg.solve_triangular(lower, jnp.eye(order, dtype=jnp.float32...  29.9 us
    pallas_call x3, Pallas kernels, kernel_product(): pl.pallas_call(functools.partial(product_body, min(256, keys)), grid=(row...  23.1 us
  transfers between devices with their start and end apart: 8, of which 7 were waited for; matrix products, arithmetic and copies ran while one was open for 4% of the time, Pallas kernels for 0%

profile of v1, /device:TPU:1, one launch (start us, length us, event | category | flops | bytes accessed | tf_op | source)
XLA Modules:
  0.0 732.8 jit_solution(11778753350643327227)
XLA Ops:
  3.3 11.9 %all-to-all-start = ((f32[16,160,128]{2,1,0:T(8,128)}), f32[16,160,128]{2,1,0:T(8,128)S(1)}, u32[]{:S(2)}, u32[]{:S(2)}) async-start(f32[16,160,128]{2,1,0:T(8,128)} %broadcast_in_dim.29), calls=%async_computation | async-start | bytes 2621440 | tf_op jit(solution)/shard_map/all_to_all | solution.py:23
  16.0 30.6 %all-to-all-done = f32[16,160,128]{2,1,0:T(8,128)S(1)} async-done(((f32[16,160,128]{2,1,0:T(8,128)}), f32[16,160,128]{2,1,0:T(8,128)S(1)}, u32[]{:S(2)}, u32[]{:S(2)}) %all-to-all-start) | async-done | bytes 1310752 | tf_op jit(solution)/shard_map/all_to_all | solution.py:23
  49.7 9.6 %all-to-all-start.1 = ((bf16[16,160,128]{2,1,0:T(8,128)(2,1)}), bf16[16,160,128]{2,1,0:T(8,128)(2,1)S(1)}, u32[]{:S(2)}, u32[]{:S(2)}) async-start(bf16[16,160,128]{2,1,0:T(8,128)(2,1)} %pad_maximum_fusion.2), calls=%async_computation.1 | async-start | bytes 1310720 | tf_op jit(solution)/shard_map/all_to_all | solution.py:23
  100.1 11.7 %cholesky.286 = f32[128,128]{1,0:T(8,128)S(1)} custom-call(f32[128,128]{1,0:T(8,128)S(1)} %cholesky.426), custom_call_target="Cholesky" | custom-call | tf_op jit(solution)/shard_map/jit(cholesky)/cholesky | solution.py:102
  112.4 10.6 %custom-call.27 = f32[1,128,128]{1,2,0:T(8,128)S(1)} custom-call(f32[1,128,128]{2,1,0:T(8,128)} %get-tuple-element.134), custom_call_target="InvertDiagBlocksLowerTriangular" | custom-call | tf_op jit(solution)/shard_map/jit(cholesky)/cholesky | solution.py:102
  128.1 12.1 %cholesky.305 = f32[128,128]{1,0:T(8,128)S(1)} custom-call(f32[128,128]{1,0:T(8,128)S(1)} %cholesky.430), custom_call_target="Cholesky" | custom-call | tf_op jit(solution)/shard_map/jit(cholesky)/cholesky | solution.py:102
  140.8 9.8 %custom-call.28 = f32[1,128,128]{1,2,0:T(8,128)S(1)} custom-call(f32[1,128,128]{2,1,0:T(8,128)S(1)} %get-tuple-element.131), custom_call_target="InvertDiagBlocksLowerTriangular" | custom-call | tf_op jit(solution)/shard_map/jit(cholesky)/cholesky | solution.py:102
  154.5 13.2 %cholesky.326 = f32[128,128]{1,0:T(8,128)} custom-call(f32[128,128]{1,0:T(8,128)} %cholesky.435), custom_call_target="Cholesky" | custom-call | tf_op jit(solution)/shard_map/jit(cholesky)/cholesky | solution.py:102
  169.8 11.3 %custom-call.29 = f32[1,128,128]{1,2,0:T(8,128)} custom-call(f32[1,128,128]{2,1,0:T(8,128)} %get-tuple-element.128), custom_call_target="InvertDiagBlocksLowerTriangular" | custom-call | tf_op jit(solution)/shard_map/jit(cholesky)/cholesky | solution.py:102
  184.2 11.9 %cholesky.343 = f32[128,128]{1,0:T(8,128)S(1)} custom-call(f32[128,128]{1,0:T(8,128)S(1)} %convolution_subtract_fusion.14), custom_call_target="Cholesky" | custom-call | tf_op jit(solution)/shard_map/jit(cholesky)/cholesky | solution.py:102
  203.5 14.0 %while.8 = (s32[]{:T(128)}, f32[512,512]{1,0:T(8,128)}, s32[4,2]{0,1:T(2,128)S(1)}, f32[4,128,128]{2,1,0:T(8,128)}, s32[]{:T(128)}) while((s32[]{:T(128)}, f32[512,512]{1,0:T(8,128)}, s32[4,2]{0,1:T(2,128)S(1)}, f32[4,128,128]{2,1,0:T(8,128)}, s32[]{:T(128)}) %tuple.96), condition=%wide.while_cond.4, body=%wide.while_body.4.sunk | while | flops 2 | bytes 132205 | solution.py:103
  217.5 40.7 %custom-call.30 = f32[4,128,128]{1,2,0:T(8,128)} custom-call(f32[4,128,128]{2,1,0:T(8,128)} %get-tuple-element.67), custom_call_target="InvertDiagBlocksLowerTriangular" | custom-call | tf_op jit(solution)/shard_map/jit(_solve_triangular)/triangular_solve | solution.py:103
  277.3 8.5 %fusion.131 = f32[512,512]{1,0:T(8,128)} fusion(f32[2048,512]{1,0:T(8,128)S(1)} %fusion), kind=kOutput, calls=%fused_computation.296 | convolution fusion | flops 6442450944 | bytes 5242880 | tf_op jit(solution)/shard_map/dot_general | solution.py:160
  299.1 16.9 %all-to-all-done.3 = f32[16,144,128]{2,1,0:T(8,128)} async-done(((f32[16,144,128]{2,1,0:T(8,128)}), f32[16,144,128]{2,1,0:T(8,128)}, u32[]{:S(2)}, u32[]{:S(2)}) %all-to-all-start.3) | async-done | bytes 1179680 | tf_op jit(solution)/shard_map/all_to_all | solution.py:23
  357.1 11.7 %cholesky.358 = f32[128,128]{1,0:T(8,128)S(1)} custom-call(f32[128,128]{1,0:T(8,128)S(1)} %cholesky.439), custom_call_target="Cholesky" | custom-call | tf_op jit(solution)/shard_map/jit(cholesky)/cholesky | solution.py:102
  370.1 10.6 %custom-call.31 = f32[1,128,128]{1,2,0:T(8,128)S(1)} custom-call(f32[1,128,128]{2,1,0:T(8,128)} %get-tuple-element.124), custom_call_target="InvertDiagBlocksLowerTriangular" | custom-call | tf_op jit(solution)/shard_map/jit(cholesky)/cholesky | solution.py:102
  385.8 11.7 %cholesky.377 = f32[128,128]{1,0:T(8,128)S(1)} custom-call(f32[128,128]{1,0:T(8,128)S(1)} %cholesky.443), custom_call_target="Cholesky" | custom-call | tf_op jit(solution)/shard_map/jit(cholesky)/cholesky | solution.py:102
  398.8 10.0 %custom-call.32 = f32[1,128,128]{1,2,0:T(8,128)S(1)} custom-call(f32[1,128,128]{2,1,0:T(8,128)S(1)} %get-tuple-element.121), custom_call_target="InvertDiagBlocksLowerTriangular" | custom-call | tf_op jit(solution)/shard_map/jit(cholesky)/cholesky | solution.py:102
  412.7 13.2 %cholesky.398 = f32[128,128]{1,0:T(8,128)} custom-call(f32[128,128]{1,0:T(8,128)} %cholesky.448), custom_call_target="Cholesky" | custom-call | tf_op jit(solution)/shard_map/jit(cholesky)/cholesky | solution.py:102
  427.9 11.3 %custom-call.33 = f32[1,128,128]{1,2,0:T(8,128)} custom-call(f32[1,128,128]{2,1,0:T(8,128)} %get-tuple-element.118), custom_call_target="InvertDiagBlocksLowerTriangular" | custom-call | tf_op jit(solution)/shard_map/jit(cholesky)/cholesky | solution.py:102
  442.3 12.1 %cholesky.415 = f32[128,128]{1,0:T(8,128)S(1)} custom-call(f32[128,128]{1,0:T(8,128)S(1)} %convolution_subtract_fusion.13), custom_call_target="Cholesky" | custom-call | tf_op jit(solution)/shard_map/jit(cholesky)/cholesky | solution.py:102
  461.2 14.4 %while.9 = (s32[]{:T(128)}, f32[512,512]{1,0:T(8,128)}, s32[4,2]{0,1:T(2,128)S(1)}, f32[4,128,128]{2,1,0:T(8,128)}, s32[]{:T(128)}) while((s32[]{:T(128)}, f32[512,512]{1,0:T(8,128)}, s32[4,2]{0,1:T(2,128)S(1)}, f32[4,128,128]{2,1,0:T(8,128)}, s32[]{:T(128)}) %tuple.102), condition=%wide.while_cond.4.clone, body=%wide.while_body.4.clone.sunk | while | flops 2 | bytes 132205 | solution.py:103
  475.7 40.7 %custom-call.34 = f32[4,128,128]{1,2,0:T(8,128)} custom-call(f32[4,128,128]{2,1,0:T(8,128)} %get-tuple-element.68), custom_call_target="InvertDiagBlocksLowerTriangular" | custom-call | tf_op jit(solution)/shard_map/jit(_solve_triangular)/triangular_solve | solution.py:103
  534.9 7.8 %kernel_product.3 = f32[32,2048]{1,0:T(8,128)S(1)} custom-call(bf16[2048,256]{1,0:T(8,128)(2,1)S(1)} %concatenate.59.key_ref, bf16[2048,256]{1,0:T(8,128)(2,1)S(1)} %concatenate.64.row_ref, bf16[96,2048]{1,0:T(8,128)(2,1)S(1)} %pad_maximum_fusion.3.parts_ref), custom_call_target="tpu_custom_call" | custom-call | tf_op jit(solution)/shard_map/kernel_product/pallas_call | solution.py:84
  555.9 15.5 %all_to_all.70 = f32[16,32,128]{2,1,0:T(8,128)S(1)} all-to-all(f32[16,32,128]{2,1,0:T(8,128)S(1)} %broadcast_in_dim.36), channel_id=1, replica_groups=mesh['x'=4,'z'=8,'yh'=2,'yl'=2,'c'=2] {'z','yh'}, dimensions={0} | all-to-all | bytes 524288 | tf_op jit(solution)/shard_map/all_to_all | solution.py:23
  585.5 15.9 %all-to-all-done.7 = f32[16,136,128]{2,1,0:T(8,128)} async-done(((f32[16,136,128]{2,1,0:T(8,128)}), f32[16,136,128]{2,1,0:T(8,128)}, u32[]{:S(2)}, u32[]{:S(2)}) %all-to-all-start.7) | async-done | bytes 1114144 | tf_op jit(solution)/shard_map/all_to_all | solution.py:23
  621.4 11.2 %all_to_all.72 = f32[16,32,128]{2,1,0:T(8,128)S(1)} all-to-all(f32[16,32,128]{2,1,0:T(8,128)S(1)} %bitcast_bitcast_fusion.1), channel_id=1, replica_groups=mesh['x'=4,'z'=8,'yh'=2,'yl'=2,'c'=2] {'x','yl','c'}, dimensions={0} | all-to-all | bytes 524288 | tf_op jit(solution)/shard_map/all_to_all | solution.py:23
  633.4 15.6 %all_to_all.71 = f32[16,32,128]{2,1,0:T(8,128)S(1)} all-to-all(f32[16,32,128]{2,1,0:T(8,128)S(1)} %broadcast_in_dim.38), channel_id=1, replica_groups=mesh['x'=4,'z'=8,'yh'=2,'yl'=2,'c'=2] {'z','yh'}, dimensions={0} | all-to-all | bytes 524288 | tf_op jit(solution)/shard_map/all_to_all | solution.py:23
  656.2 22.3 %all_to_all.73 = f32[16,136,128]{2,1,0:T(8,128)} all-to-all(f32[16,136,128]{2,1,0:T(8,128)S(1)} %broadcast_in_dim.39), channel_id=1, replica_groups=mesh['x'=4,'z'=8,'yh'=2,'yl'=2,'c'=2] {'x','yl','c'}, dimensions={0} | all-to-all | bytes 2228224 | tf_op jit(solution)/shard_map/all_to_all | solution.py:23
  697.7 10.3 %all_to_all.74 = f32[16,32,128]{2,1,0:T(8,128)S(1)} all-to-all(f32[16,32,128]{2,1,0:T(8,128)S(1)} %bitcast_bitcast_fusion), channel_id=1, replica_groups=mesh['x'=4,'z'=8,'yh'=2,'yl'=2,'c'=2] {'x','yl','c'}, dimensions={0} | all-to-all | bytes 524288 | tf_op jit(solution)/shard_map/all_to_all | solution.py:23
  708.8 8.7 %all_to_all.75 = f32[16,8,128]{2,1,0:T(8,128)S(1)} all-to-all(f32[16,8,128]{2,1,0:T(8,128)S(1)} %broadcast_in_dim.41), channel_id=1, replica_groups=mesh['x'=4,'z'=8,'yh'=2,'yl'=2,'c'=2] {'x','yl','c'}, dimensions={0} | all-to-all | bytes 131072 | tf_op jit(solution)/shard_map/all_to_all | solution.py:23
  723.3 7.8 %all-to-all-done.13 = f32[16,8,128]{2,1,0:T(8,128)S(1)} async-done(((f32[16,8,128]{2,1,0:T(8,128)}), f32[16,8,128]{2,1,0:T(8,128)S(1)}, u32[]{:S(2)}, u32[]{:S(2)}) %all-to-all-start.13) | async-done | bytes 65568 | tf_op jit(solution)/shard_map/all_to_all | solution.py:23
  (265 shorter events, 291.0 us)
Async XLA Ops:
  0.6 14.6 %copy-start.22 = (s32[2,256]{1,0:T(2,128)S(1)}, s32[2,256]{1,0:T(2,128)}, u32[]{:S(2)}) copy-start(s32[2,256]{1,0:T(2,128)} %param.16) | copy-start | bytes 6148
  3.3 45.4 %copy-start.21 = (bf16[128,128]{1,0:T(8,128)(2,1)S(1)}, bf16[128,128]{1,0:T(8,128)(2,1)}, u32[]{:S(2)}) copy-start(bf16[128,128]{1,0:T(8,128)(2,1)} %param.14) | copy-start | bytes 98308
  3.3 43.3 %all-to-all-start = ((f32[16,160,128]{2,1,0:T(8,128)}), f32[16,160,128]{2,1,0:T(8,128)S(1)}, u32[]{:S(2)}, u32[]{:S(2)}) async-start(f32[16,160,128]{2,1,0:T(8,128)} %broadcast_in_dim.29), calls=%async_computation | async-start | bytes 2621440 | tf_op jit(solution)/shard_map/all_to_all | solution.py:23
  16.0 249.5 %copy-start.4 = (f32[512,512]{0,1:T(8,128)}, f32[512,512]{0,1:T(8,128)S(1)}, u32[]{:S(2)}) copy-start(f32[512,512]{0,1:T(8,128)S(1)} %fusion.25) | copy-start | bytes 3145732
  46.6 483.5 %copy-start.3 = (f32[16,160,128]{2,1,0:T(8,128)}, f32[16,160,128]{2,1,0:T(8,128)S(1)}, u32[]{:S(2)}) copy-start(f32[16,160,128]{2,1,0:T(8,128)S(1)} %all-to-all-done) | copy-start | bytes 3932164
  49.7 20.4 %all-to-all-start.1 = ((bf16[16,160,128]{2,1,0:T(8,128)(2,1)}), bf16[16,160,128]{2,1,0:T(8,128)(2,1)S(1)}, u32[]{:S(2)}, u32[]{:S(2)}) async-start(bf16[16,160,128]{2,1,0:T(8,128)(2,1)} %pad_maximum_fusion.2), calls=%async_computation.1 | async-start | bytes 1310720 | tf_op jit(solution)/shard_map/all_to_all | solution.py:23
  70.1 7.7 %copy-start.5 = (bf16[16,160,128]{2,1,0:T(8,128)(2,1)}, bf16[16,160,128]{2,1,0:T(8,128)(2,1)S(1)}, u32[]{:S(2)}) copy-start(bf16[16,160,128]{2,1,0:T(8,128)(2,1)S(1)} %all-to-all-done.1) | copy-start | bytes 1966084
  70.9 11.2 %all-to-all-start.2 = ((bf16[16,32,128]{2,1,0:T(8,128)(2,1)}), bf16[16,32,128]{2,1,0:T(8,128)(2,1)S(1)}, u32[]{:S(2)}, u32[]{:S(2)}) async-start(bf16[16,32,128]{2,1,0:T(8,128)(2,1)} %broadcast_in_dim.31), calls=%async_computation.2 | async-start | bytes 262144 | tf_op jit(solution)/shard_map/all_to_all | solution.py:23
  99.0 1.0 copy-start.10
  100.0 102.8 %copy-start.23 = (s32[4]{0:T(128)S(1)}, s32[4]{0:T(128)}, u32[]{:S(2)}) copy-start(s32[4]{0:T(128)} %iota_multiply_fusion) | copy-start | bytes 52
  127.4 0.7 copy-start.18
  258.3 10.9 %copy-start.15 = (bf16[512,256]{1,0:T(8,128)(2,1)S(1)}, bf16[512,256]{1,0:T(8,128)(2,1)}, u32[]{:S(2)}) copy-start(bf16[512,256]{1,0:T(8,128)(2,1)} %concatenate.61) | copy-start | bytes 786436
  277.3 8.5 %copy-start = (f32[2048,512]{1,0:T(8,128)}, f32[2048,512]{1,0:T(8,128)S(1)}, u32[]{:S(2)}) copy-start(f32[2048,512]{1,0:T(8,128)S(1)} %fusion) | copy-start | bytes 12582916
  288.3 10.5 %copy-start.6 = (bf16[16,160,128]{2,1,0:T(8,128)(2,1)S(1)}, bf16[16,160,128]{2,1,0:T(8,128)(2,1)}, u32[]{:S(2)}) copy-start(bf16[16,160,128]{2,1,0:T(8,128)(2,1)} %copy-done.5) | copy-start | bytes 1966084
  293.0 23.0 %all-to-all-start.3 = ((f32[16,144,128]{2,1,0:T(8,128)}), f32[16,144,128]{2,1,0:T(8,128)}, u32[]{:S(2)}, u32[]{:S(2)}) async-start(f32[16,144,128]{2,1,0:T(8,128)} %pad_maximum_fusion), calls=%async_computation.3 | async-start | bytes 2359296 | tf_op jit(solution)/shard_map/all_to_all | solution.py:23
  318.4 22.3 %all-to-all-start.4 = ((f32[16,144,128]{2,1,0:T(8,128)}), f32[16,144,128]{2,1,0:T(8,128)}, u32[]{:S(2)}, u32[]{:S(2)}) async-start(f32[16,144,128]{2,1,0:T(8,128)} %broadcast_in_dim.35), calls=%async_computation.4 | async-start | bytes 2359296 | tf_op jit(solution)/shard_map/all_to_all | solution.py:23
  356.1 1.0 copy-start.9
  385.1 0.7 copy-start.17
  458.1 70.1 %copy-start.19 = (f32[32,512]{1,0:T(8,128)S(1)}, f32[32,512]{1,0:T(8,128)}, u32[]{:S(2)}) copy-start(f32[32,512]{1,0:T(8,128)} %reshape.425) | copy-start | bytes 196612
  517.8 12.3 %copy-start.7 = (f32[128,512]{1,0:T(8,128)}, f32[128,512]{1,0:T(8,128)S(1)}, u32[]{:S(2)}) copy-start(f32[128,512]{1,0:T(8,128)S(1)} %fusion.63) | copy-start | bytes 786436
  519.5 10.6 %copy-start.1 = (f32[2048,512]{1,0:T(8,128)S(1)}, f32[2048,512]{1,0:T(8,128)}, u32[]{:S(2)}) copy-start(f32[2048,512]{1,0:T(8,128)} %copy-done) | copy-start | bytes 12582916
  520.9 8.4 %copy-start.12 = (f32[128,512]{1,0:T(8,128)}, f32[128,512]{1,0:T(8,128)S(1)}, u32[]{:S(2)}) copy-start(f32[128,512]{1,0:T(8,128)S(1)} %fusion.87) | copy-start | bytes 786436
  524.3 5.8 copy-start.16
  528.2 1.9 copy-start.20
  542.8 34.5 %copy-start.14 = (f32[32,2048]{1,0:T(8,128)S(1)}, f32[32,2048]{1,0:T(8,128)}, u32[]{:S(2)}) copy-start(f32[32,2048]{1,0:T(8,128)} %get-tuple-element.146) | copy-start | bytes 786436
  543.5 11.6 %all-to-all-start.5 = ((f32[16,32,128]{2,1,0:T(8,128)}), f32[16,32,128]{2,1,0:T(8,128)S(1)}, u32[]{:S(2)}, u32[]{:S(2)}) async-start(f32[16,32,128]{2,1,0:T(8,128)} %bitcast_bitcast_fusion.2), calls=%async_computation.5 | async-start | bytes 524288 | tf_op jit(solution)/shard_map/all_to_all | solution.py:23
  576.1 26.8 %copy-start.8 = (f32[128,512]{1,0:T(8,128)S(1)}, f32[128,512]{1,0:T(8,128)}, u32[]{:S(2)}) copy-start(f32[128,512]{1,0:T(8,128)} %copy-done.7) | copy-start | bytes 786436
  576.1 26.8 %copy-start.13 = (f32[128,512]{1,0:T(8,128)S(1)}, f32[128,512]{1,0:T(8,128)}, u32[]{:S(2)}) copy-start(f32[128,512]{1,0:T(8,128)} %copy-done.12) | copy-start | bytes 786436
  578.7 22.8 %all-to-all-start.7 = ((f32[16,136,128]{2,1,0:T(8,128)}), f32[16,136,128]{2,1,0:T(8,128)}, u32[]{:S(2)}, u32[]{:S(2)}) async-start(f32[16,136,128]{2,1,0:T(8,128)} %broadcast_in_dim.37), calls=%async_computation.7 | async-start | bytes 2228224 | tf_op jit(solution)/shard_map/all_to_all | solution.py:23
  656.2 29.1 %copy-start.11 = (f32[32,2048]{1,0:T(8,128)S(1)}, f32[32,2048]{1,0:T(8,128)}, u32[]{:S(2)}) copy-start(f32[32,2048]{1,0:T(8,128)} %get-tuple-element.151) | copy-start | bytes 786436
  679.8 5.5 copy-start.2
  718.2 12.9 %all-to-all-start.13 = ((f32[16,8,128]{2,1,0:T(8,128)}), f32[16,8,128]{2,1,0:T(8,128)S(1)}, u32[]{:S(2)}, u32[]{:S(2)}) async-start(f32[16,8,128]{2,1,0:T(8,128)} %broadcast_in_dim.42), calls=%async_computation.13 | async-start | bytes 131072 | tf_op jit(solution)/shard_map/all_to_all | solution.py:23
